TPU v7x, 32 devices: a whole 2x2x4 slice. The times are simulated.
32 devices in a mesh: expert: 8 (over y, x, core), dp: 4 (over z).
Axes of the slice: x: 2, y: 2, z: 4, core: 2. Of those that a mesh axis runs over, the one named last changes fastest.
Arguments:
- trunk: bfloat16 [768, 4096], P(('dp', 'expert')), may hold values from -6 to 6
- w_first: bfloat16 [8, 4096, 2048], P('expert'), may hold values from -0.09375 to 0.09375
- w_second: bfloat16 [8, 2048, 1024], P('expert'), may hold values from -0.125 to 0.125
- gates: bfloat16 [8, 8, 768], P('expert', None, 'dp'), may hold values from 0.049804688 to 1
- d_mixed: bfloat16 [768, 8, 1024], P(('dp', 'expert')), may hold values from -6 to 6
Outputs:
- mixed: bfloat16 [768, 8, 1024], P(('dp', 'expert'))
- d_trunk: bfloat16 [768, 4096], P(('dp', 'expert'))
- d_gates: bfloat16 [8, 8, 768], P('expert', None, 'dp')
- d_w_first: bfloat16 [8, 4096, 2048], P('expert', 'dp')
- d_w_second: bfloat16 [8, 2048, 1024], P('expert', 'dp')
All inputs are finite; a program needn't handle non-finite values.
Results may differ from a plain program's by a relative error of at most 0.015.
Values may be sent and summed in bfloat16 or wider, within the bound.
A program may use at most 128 MiB of HBM per device.

v0:
```python
import jax
import jax.numpy as jnp
from jax import lax
from jax.sharding import PartitionSpec as P


def on_device(trunk, w_first, w_second, gates, d_mixed):
    rows_all = lax.all_gather(trunk, "expert", axis=0, tiled=True)
    first = w_first[0]
    second = w_second[0]
    gate_here = gates[0]
    pre = jnp.dot(rows_all, first, preferred_element_type=jnp.float32)
    hidden = jax.nn.silu(pre).astype(jnp.bfloat16)
    output = jnp.dot(hidden, second, preferred_element_type=jnp.float32).astype(jnp.bfloat16)
    outs_each, gates_each = (
        lax.all_to_all(output[None], "expert", split_axis=1, concat_axis=0, tiled=True),
        lax.all_to_all(gate_here.T[None], "expert", split_axis=1, concat_axis=0, tiled=True),
    )
    mixed = jnp.einsum(
        "ert,ero->rto", gates_each, outs_each, preferred_element_type=jnp.float32
    ).astype(jnp.bfloat16)
    d_out_each = jnp.einsum(
        "ert,rto->ero", gates_each, d_mixed, preferred_element_type=jnp.float32
    ).astype(jnp.bfloat16)
    d_gate_each = jnp.einsum(
        "rto,ero->ert", d_mixed, outs_each, preferred_element_type=jnp.float32
    ).astype(jnp.bfloat16)
    back_out, back_gate = (
        lax.all_to_all(d_out_each, "expert", split_axis=0, concat_axis=1, tiled=True),
        lax.all_to_all(d_gate_each, "expert", split_axis=0, concat_axis=1, tiled=True),
    )
    d_output = back_out[0]
    d_gate = back_gate[0].T[None]
    d_hidden = lax.dot_general(
        d_output, second, (((1,), (1,)), ((), ())), preferred_element_type=jnp.float32
    )
    sig = jax.nn.sigmoid(pre)
    d_pre = (d_hidden * sig * (1.0 + pre * (1.0 - sig))).astype(jnp.bfloat16)
    piece = d_pre
    d_trunk = lax.psum_scatter(
        lax.dot_general(
            piece, first, (((1,), (1,)), ((), ())), preferred_element_type=jnp.float32
        ).astype(jnp.bfloat16),
        "expert",
        scatter_dimension=0,
        tiled=True,
    )
    piece = rows_all
    d_first = lax.psum_scatter(
        lax.dot_general(
            piece, d_pre, (((0,), (0,)), ((), ())), preferred_element_type=jnp.float32
        ).astype(jnp.bfloat16),
        "dp",
        scatter_dimension=0,
        tiled=True,
    )
    piece = hidden
    d_second = lax.psum_scatter(
        lax.dot_general(
            piece, d_output, (((0,), (0,)), ((), ())), preferred_element_type=jnp.float32
        ).astype(jnp.bfloat16),
        "dp",
        scatter_dimension=0,
        tiled=True,
    )
    return (mixed, d_trunk, d_gate, d_first[None], d_second[None])


def solution(mesh):
    in_specs = (
        P(("dp", "expert"), None),
        P("expert", None, None),
        P("expert", None, None),
        P("expert", None, "dp"),
        P(("dp", "expert"), None, None),
    )
    out_specs = (
        P(("dp", "expert"), None, None),
        P(("dp", "expert"), None),
        P("expert", None, "dp"),
        P("expert", "dp", None),
        P("expert", "dp", None),
    )
    return jax.shard_map(
        on_device, mesh=mesh, in_specs=in_specs, out_specs=out_specs, check_vma=False
    )
```

profile of v0, /device:TPU:11, one launch (start us, length us, event | category | flops | bytes accessed | tf_op | source)
XLA Modules:
  0.0 469.6 jit_solution(6701005433292984852)
XLA Ops:
  7.2 0.0 copy-start
  7.2 0.0 all-gather.2.cloned.1.call-start
  7.2 0.7 all-gather.2.cloned.1.call-update
  7.9 0.8 copy.31
  8.7 7.8 %all_to_all.42 = bf16[1,192,8]{2,0,1:T(2,128)(2,1)S(1)} all-to-all(bf16[1,192,8]{2,0,1:T(2,128)(2,1)S(1)} %copy.31), channel_id=1, replica_groups=mesh['expert'=8,'dp'=4] {'expert'}, dimensions={1} | all-to-all | bytes 6144 | tf_op jit(solution)/shard_map/all_to_all | solution.py:17
  16.5 0.1 copy.32
  16.6 0.1 all_to_all.15
  16.7 0.1 copy.35
  16.8 0.0 copy-done
  16.8 0.3 fusion.24
  17.1 1.0 copy.36
  18.1 5.1 %all-to-all-start.2 = ((bf16[8,24,1024]{2,1,0:T(8,128)(2,1)}), bf16[8,24,1024]{2,1,0:T(8,128)(2,1)S(1)}, u32[]{:S(2)}, u32[]{:S(2)}) async-start(bf16[8,24,1024]{2,1,0:T(8,128)(2,1)} %copy.36), calls=%async_computation.2 | async-start | bytes 786432 | tf_op jit(solution)/shard_map/all_to_all | solution.py:29
  23.2 0.0 reduce-scatter.6.cloned.1.call-start
  23.2 13.8 %all-gather.2.cloned.1.call-done = bf16[192,4096]{1,0:T(8,128)(2,1)} async-done(((bf16[24,4096]{1,0:T(8,128)(2,1)}), bf16[192,4096]{1,0:T(8,128)(2,1)}) %all-gather.2.cloned.1.call-update) | async-done | bytes 1572880 | tf_op jit(solution)/shard_map/all_gather | solution.py:8
  37.0 10.8 %fusion.2 = f32[192,2048]{1,0:T(8,128)} fusion(bf16[192,4096]{1,0:T(8,128)(2,1)} %all-gather.2.cloned.1.call-done, bf16[1,4096,2048]{2,1,0:T(8,128)(2,1)} %param.6), kind=kOutput, calls=%fused_computation.2 | convolution fusion | flops 3221225472 | bytes 19922944 | tf_op jit(solution)/shard_map/dot_general | solution.py:12
  47.8 0.0 all-to-all-done.2
  47.8 0.0 copy-start.1
  47.8 4.5 fusion.17
  52.3 0.0 copy-done.1
  52.4 8.1 %convert_bitcast_fusion = bf16[4096,2048]{0,1:T(8,128)(2,1)} fusion(bf16[192,2048]{1,0:T(8,128)(2,1)S(1)} %fusion.17, bf16[192,4096]{1,0:T(8,128)(2,1)S(1)} %copy-done.1), kind=kOutput, calls=%fused_computation.4 | convolution fusion | flops 3229614080 | bytes 19136512 | tf_op jit(solution)/shard_map/dot_general | solution.py:50
  60.5 0.0 reduce-scatter.6.cloned.1.call-update
  60.5 0.0 reduce-scatter.4.cloned.1.call-start
  60.6 12.6 %fusion.4 = bf16[192,4096]{1,0:T(8,128)(2,1)} fusion(bf16[192,2048]{1,0:T(8,128)(2,1)S(1)} %fusion.17, bf16[1,4096,2048]{2,1,0:T(8,128)(2,1)} %param.6), kind=kOutput, calls=%fused_computation.5 | convolution fusion | flops 3222011904 | bytes 19136512 | tf_op jit(solution)/shard_map/dot_general | solution.py:41
  73.2 0.0 copy-start.2
  73.2 0.0 reduce-scatter.4.cloned.1.call-update
  73.2 0.2 reduce-scatter.8.cloned.1.call-start
  73.4 1.2 copy-done.2
  74.6 3.3 convolution_convert_fusion
  77.9 0.0 reduce-scatter.8.cloned.1.call-update
  77.9 3.2 fusion.25
  81.1 0.6 copy.47
  81.8 0.5 broadcast.1
  82.3 2.9 reduce
  85.2 0.2 reshape.24
  85.5 9.6 %all_to_all.43 = bf16[8,2,12288]{2,1,0:T(2,128)(2,1)S(1)} all-to-all(bf16[8,2,12288]{2,1,0:T(2,128)(2,1)S(1)} %reshape.24), channel_id=1, replica_groups=mesh['expert'=8,'dp'=4] {'expert'}, dimensions={0} | all-to-all | bytes 786432 | tf_op jit(solution)/shard_map/all_to_all | solution.py:16
  95.0 0.4 reshape.25
  95.4 0.1 copy.41
  95.6 0.4 fusion.28
  95.9 0.7 copy.38
  96.6 5.0 %all-to-all-start.3 = ((bf16[8,24,8]{1,2,0:T(8,128)(2,1)}), bf16[8,24,8]{1,2,0:T(8,128)(2,1)S(1)}, u32[]{:S(2)}, u32[]{:S(2)}) async-start(bf16[8,24,8]{1,2,0:T(8,128)(2,1)} %copy.38), calls=%async_computation.4 | async-start | bytes 32768 | tf_op jit(solution)/shard_map/all_to_all | solution.py:30
  101.6 1.1 fusion.23
  102.7 2.3 all-to-all-done.3
  105.0 0.7 squeeze.19
  105.7 231.9 %reduce-scatter.6.cloned.1.call-done = bf16[1024,2048]{0,1:T(8,128)(2,1)} async-done(((bf16[4096,2048]{0,1:T(8,128)(2,1)}), bf16[1024,2048]{0,1:T(8,128)(2,1)}) %reduce-scatter.6.cloned.1.call-update) | async-done | bytes 4194320 | tf_op jit(solution)/shard_map/reduce_scatter | solution.py:49
  337.5 6.4 %copy.40 = bf16[1,1024,2048]{2,1,0:T(8,128)(2,1)} copy(bf16[1,1024,2048]{1,2,0:T(8,128)(2,1)} %bitcast.62) | data formatting | bytes 8388608
  343.9 39.4 %reduce-scatter.4.cloned.1.call-done = bf16[24,4096]{1,0:T(8,128)(2,1)} async-done(((bf16[192,4096]{1,0:T(8,128)(2,1)}), bf16[24,4096]{1,0:T(8,128)(2,1)}) %reduce-scatter.4.cloned.1.call-update) | async-done | bytes 196624 | tf_op jit(solution)/shard_map/reduce_scatter | solution.py:40
  383.4 79.7 %reduce-scatter.8.cloned.1.call-done = bf16[512,1024]{1,0:T(8,128)(2,1)} async-done(((bf16[2048,1024]{1,0:T(8,128)(2,1)}), bf16[512,1024]{1,0:T(8,128)(2,1)}) %reduce-scatter.8.cloned.1.call-update) | async-done | bytes 1048592 | tf_op jit(solution)/shard_map/reduce_scatter | solution.py:58
  (1 shorter events, 0.0 us)
Async XLA Ops:
  7.2 9.7 %copy-start = (bf16[24,8,1024]{2,1,0:T(8,128)(2,1)S(1)}, bf16[24,8,1024]{2,1,0:T(8,128)(2,1)}, u32[]{:S(2)}) copy-start(bf16[24,8,1024]{2,1,0:T(8,128)(2,1)} %param.9) | copy-start | bytes 1179652
  7.2 29.8 %all-gather.2.cloned.1.call-start = ((), (), s32[]{:S(2)}) async-start(), calls=%async_computation.7 | async-start | bytes 1769472 | tf_op jit(solution)/shard_map/all_gather | solution.py:8
  18.1 29.8 %all-to-all-start.2 = ((bf16[8,24,1024]{2,1,0:T(8,128)(2,1)}), bf16[8,24,1024]{2,1,0:T(8,128)(2,1)S(1)}, u32[]{:S(2)}, u32[]{:S(2)}) async-start(bf16[8,24,1024]{2,1,0:T(8,128)(2,1)} %copy.36), calls=%async_computation.2 | async-start | bytes 786432 | tf_op jit(solution)/shard_map/all_to_all | solution.py:29
  23.2 314.4 %reduce-scatter.6.cloned.1.call-start = ((), (), s32[]{:S(2)}) async-start(), calls=%async_computation.9 | async-start | bytes 20971520 | tf_op jit(solution)/shard_map/reduce_scatter | solution.py:49
  47.8 4.5 copy-start.1
  60.5 322.9 %reduce-scatter.4.cloned.1.call-start = ((), (), s32[]{:S(2)}) async-start(), calls=%async_computation.8 | async-start | bytes 1769472 | tf_op jit(solution)/shard_map/reduce_scatter | solution.py:40
  73.2 1.4 copy-start.2
  73.2 389.9 %reduce-scatter.8.cloned.1.call-start = ((), (), s32[]{:S(2)}) async-start(), calls=%async_computation.10 | async-start | bytes 5242880 | tf_op jit(solution)/shard_map/reduce_scatter | solution.py:58
  96.6 8.3 %all-to-all-start.3 = ((bf16[8,24,8]{1,2,0:T(8,128)(2,1)}), bf16[8,24,8]{1,2,0:T(8,128)(2,1)S(1)}, u32[]{:S(2)}, u32[]{:S(2)}) async-start(bf16[8,24,8]{1,2,0:T(8,128)(2,1)} %copy.38), calls=%async_computation.4 | async-start | bytes 32768 | tf_op jit(solution)/shard_map/all_to_all | solution.py:30
Sparse Core Ops, SparseCore 0:
  9.9 27.0 all-gather.1
  60.6 276.8 reduce-scatter.5
  341.4 41.9 reduce-scatter.3
  386.1 76.9 reduce-scatter.7
where the time goes:
time: 472 us; the launch traced here: 470 us
  waiting for transfers between devices  368 us (78%)
  matrix products  44.3 us (9%)
  blocking collectives  17.4 us (4%)
  between operations  13.9 us (3%)
  local copies, waits for them, and re-layouts  12.9 us (3%)
  starting transfers between devices  10.4 us (2%)
    reduce_scatter x1, waiting for transfers between devices, on_device(): lax.psum_scatter(lax.dot_general(piece, d_pre, (((0,), (0,)), ((), ())),...  232 us
    reduce_scatter x1, waiting for transfers between devices, on_device(): lax.psum_scatter(lax.dot_general(piece, d_output, (((0,), (0,)), ((), ())...  79.7 us
    reduce_scatter x1, waiting for transfers between devices, on_device(): lax.psum_scatter(lax.dot_general(piece, first, (((1,), (1,)), ((), ())),...  39.4 us
    all_gather x1, waiting for transfers between devices, on_device(): rows_all = lax.all_gather(trunk, 'expert', axis=0, tiled=True)  13.8 us
    dot_general x1, matrix products, on_device(): lax.dot_general(piece, first, (((1,), (1,)), ((), ())), preferred_element...  12.6 us
    dot_general x1, matrix products, on_device(): pre = jnp.dot(rows_all, first, preferred_element_type=jnp.float32)  10.8 us
    all_to_all x1, blocking collectives, on_device(): lax.all_to_all(output[None], 'expert', split_axis=1, concat_axis=0, tiled...  9.58 us
  transfers between devices with their start and end apart: 6, of which 5 were waited for; matrix products, arithmetic and copies ran while one was open for 10% of the time, Pallas kernels for 0%

commit v1 on v0

v1 whole, which is shorter than its diff:
```python
import jax
import jax.numpy as jnp
from jax import lax
from jax.sharding import PartitionSpec as P

F32 = jnp.float32
BF16 = jnp.bfloat16


def on_device(trunk, w_first, w_second, gates, d_mixed):
    rank = lax.axis_index("dp")
    first = w_first[0]
    second = w_second[0]
    gate_here = gates[0]
    n_dp = lax.axis_size("dp")
    depth = first.shape[0] // n_dp
    units = second.shape[0] // n_dp
    group = gate_here.shape[1]

    rows_all = lax.all_gather(trunk, ("dp", "expert"), axis=0, tiled=True)
    gates_each = lax.all_to_all(gate_here.T[None], "expert", split_axis=1, concat_axis=0, tiled=True)
    d_out_each = jnp.einsum(
        "ert,rto->ero", gates_each, d_mixed, preferred_element_type=F32
    ).astype(BF16)
    d_output = lax.all_to_all(d_out_each, "expert", split_axis=0, concat_axis=1, tiled=True)[0]
    d_output_all = lax.all_gather(d_output, "dp", axis=0, tiled=True)

    pre = jnp.dot(rows_all, first, preferred_element_type=F32)
    pre_here = lax.dynamic_slice_in_dim(pre, rank * group, group, 0)
    hidden_here = jax.nn.silu(pre_here).astype(BF16)
    output = jnp.dot(hidden_here, second, preferred_element_type=F32).astype(BF16)
    outs_each = lax.all_to_all(output[None], "expert", split_axis=1, concat_axis=0, tiled=True)

    d_hidden = lax.dot_general(
        d_output_all, second, (((1,), (1,)), ((), ())), preferred_element_type=F32
    )
    sig = jax.nn.sigmoid(pre)
    d_pre = (d_hidden * sig * (1.0 + pre * (1.0 - sig))).astype(BF16)
    d_pre_here = lax.dynamic_slice_in_dim(d_pre, rank * group, group, 0)
    d_trunk = lax.psum_scatter(
        lax.dot_general(
            d_pre_here, first, (((1,), (1,)), ((), ())), preferred_element_type=F32
        ).astype(BF16),
        "expert",
        scatter_dimension=0,
        tiled=True,
    )

    mixed = jnp.einsum(
        "ert,ero->rto", gates_each, outs_each, preferred_element_type=F32
    ).astype(BF16)
    d_gate_each = jnp.einsum(
        "rto,ero->ert", d_mixed, outs_each, preferred_element_type=F32
    ).astype(BF16)
    back_gate = lax.all_to_all(d_gate_each, "expert", split_axis=0, concat_axis=1, tiled=True)
    d_gate = back_gate[0].T[None]

    columns = lax.dynamic_slice_in_dim(rows_all, rank * depth, depth, 1)
    d_first = lax.dot_general(
        columns, d_pre, (((0,), (0,)), ((), ())), preferred_element_type=F32
    ).astype(BF16)
    some_pre = lax.dynamic_slice_in_dim(pre, rank * units, units, 1)
    some_hidden = jax.nn.silu(some_pre).astype(BF16)
    d_second = lax.dot_general(
        some_hidden, d_output_all, (((0,), (0,)), ((), ())), preferred_element_type=F32
    ).astype(BF16)
    return (mixed, d_trunk, d_gate, d_first[None], d_second[None])


def solution(mesh):
    in_specs = (
        P(("dp", "expert"), None),
        P("expert", None, None),
        P("expert", None, None),
        P("expert", None, "dp"),
        P(("dp", "expert"), None, None),
    )
    out_specs = (
        P(("dp", "expert"), None, None),
        P(("dp", "expert"), None),
        P("expert", None, "dp"),
        P("expert", "dp", None),
        P("expert", "dp", None),
    )
    return jax.shard_map(
        on_device, mesh=mesh, in_specs=in_specs, out_specs=out_specs, check_vma=False
    )
```

time: 472 us -> 189 us (0.40)
  waiting for transfers between devices: 368 us -> 79.6 us
  matrix products: 44.3 us -> 60.7 us
  blocking collectives: 17.4 us -> 7.8 us
  local copies, waits for them, and re-layouts: 12.9 us -> 7.06 us
    reduce_scatter x3 -> x1, waiting for transfers between devices: 351 us -> 3.39 us  [on_device(): lax.psum_scatter(lax.dot_general(d_pre_here, first, (((1,), (1,)), ((), (...]
    all_gather x1 -> x2, waiting for transfers between devices: 13.8 us -> 66.5 us  [the longest x1 50.8 us: on_device(): rows_all = lax.all_gather(trunk, ('dp', 'expert'), axis=0, tiled=True)]
    dot_general x8, matrix products: 43.2 us -> 59.5 us  [the longest x1 20.2 us: on_device(): pre = jnp.dot(rows_all, first, preferred_element_type=F32)]
    all_to_all x1 -> x0, blocking collectives: 9.58 us -> none  [on_device(): lax.all_to_all(output[None], 'expert', split_axis=1, concat_axis=0, tiled...]
    all_to_all x1, waiting for transfers between devices: 0.01 us -> 6.8 us  [on_device(): lax.all_to_all(d_out_each, 'expert', split_axis=0, concat_axis=1, tiled=T...]
    unnamed x11 -> x10, local copies, waits for them, and re-layouts: 8.85 us -> 2.99 us
    all_to_all x0 -> x1, starting transfers between devices: none -> 5.01 us  [on_device(): lax.all_to_all(output[None], 'expert', split_axis=1, concat_axis=0, tiled...]
  transfers between devices with their start and end apart: 6 -> 6, of which waited for: 5 -> 5; matrix products, arithmetic and copies ran while one was open for 10% -> 25% of each run, Pallas kernels for 0% -> 0%
where the time goes in v1:
time: 189 us; the launch traced here: 186 us
  waiting for transfers between devices  79.6 us (42%)
  matrix products  60.7 us (32%)
  starting transfers between devices  14.4 us (8%)
  between operations  13.8 us (7%)
  blocking collectives  7.8 us (4%)
  local copies, waits for them, and re-layouts  7.06 us (4%)
  other arithmetic  2.92 us (2%)
    all_gather x1, waiting for transfers between devices, on_device(): rows_all = lax.all_gather(trunk, ('dp', 'expert'), axis=0, tiled=True)  50.8 us
    dot_general x1, matrix products, on_device(): pre = jnp.dot(rows_all, first, preferred_element_type=F32)  20.2 us
    all_gather x1, waiting for transfers between devices, on_device(): d_output_all = lax.all_gather(d_output, 'dp', axis=0, tiled=True)  15.7 us
    dot_general x1, matrix products, on_device(): lax.dot_general(d_pre_here, first, (((1,), (1,)), ((), ())), preferred_el...  12.8 us
    dot_general x1, matrix products, on_device(): lax.dot_general(d_output_all, second, (((1,), (1,)), ((), ())), preferred...  10.8 us
    dot_general x1, matrix products, on_device(): lax.dot_general(columns, d_pre, (((0,), (0,)), ((), ())), preferred_eleme...  7.98 us
    all_to_all x1, blocking collectives, on_device(): lax.all_to_all(gate_here.T[None], 'expert', split_axis=1, concat_axis=0,...  7.8 us
    all_to_all x1, waiting for transfers between devices, on_device(): lax.all_to_all(d_out_each, 'expert', split_axis=0, concat_axis=1, tiled=T...  6.8 us
  transfers between devices with their start and end apart: 6, of which 5 were waited for; matrix products, arithmetic and copies ran while one was open for 25% of the time, Pallas kernels for 0%

profile of v1, /device:TPU:11, one launch (start us, length us, event | category | flops | bytes accessed | tf_op | source)
XLA Modules:
  0.0 186.2 jit_solution(14458525638862660231)
XLA Ops:
  7.2 0.0 copy-start
  7.2 0.0 all-gather.3.cloned.1.call-start
  7.2 0.7 all-gather.3.cloned.1.call-update
  7.9 0.8 copy.28
  8.7 7.8 %all_to_all.42 = bf16[1,192,8]{2,0,1:T(2,128)(2,1)S(1)} all-to-all(bf16[1,192,8]{2,0,1:T(2,128)(2,1)S(1)} %copy.28), channel_id=1, replica_groups=mesh['expert'=8,'dp'=4] {'expert'}, dimensions={1} | all-to-all | bytes 6144 | tf_op jit(solution)/shard_map/all_to_all | solution.py:21
  16.5 0.1 copy.29
  16.6 0.1 all_to_all.15
  16.7 0.1 copy.32
  16.8 0.0 copy-done
  16.8 0.2 fusion.19
  17.1 1.0 copy.33
  18.1 5.1 %all-to-all-start.2 = ((bf16[8,24,1024]{2,1,0:T(8,128)(2,1)}), bf16[8,24,1024]{2,1,0:T(8,128)(2,1)S(1)}, u32[]{:S(2)}, u32[]{:S(2)}) async-start(bf16[8,24,1024]{2,1,0:T(8,128)(2,1)} %copy.33), calls=%async_computation.2 | async-start | bytes 786432 | tf_op jit(solution)/shard_map/all_to_all | solution.py:25
  23.2 0.0 all-gather.5.cloned.1.call-start
  23.2 6.8 %all-to-all-done.2 = bf16[8,24,1024]{2,1,0:T(8,128)(2,1)S(1)} async-done(((bf16[8,24,1024]{2,1,0:T(8,128)(2,1)}), bf16[8,24,1024]{2,1,0:T(8,128)(2,1)S(1)}, u32[]{:S(2)}, u32[]{:S(2)}) %all-to-all-start.2) | async-done | bytes 393248 | tf_op jit(solution)/shard_map/all_to_all | solution.py:25
  30.0 0.0 copy-start.1
  30.0 0.7 copy-done.1
  30.7 0.0 all-gather.5.cloned.1.call-update
  30.7 0.0 reduce-scatter.2.cloned.1.call-start
  30.8 50.8 %all-gather.3.cloned.1.call-done = bf16[768,4096]{1,0:T(8,128)(2,1)} async-done(((bf16[24,4096]{1,0:T(8,128)(2,1)}), bf16[768,4096]{1,0:T(8,128)(2,1)}) %all-gather.3.cloned.1.call-update) | async-done | bytes 6291472 | tf_op jit(solution)/shard_map/all_gather | solution.py:20
  81.6 20.2 %fusion.2 = f32[768,2048]{1,0:T(8,128)} fusion(bf16[768,4096]{1,0:T(8,128)(2,1)} %all-gather.3.cloned.1.call-done, bf16[1,4096,2048]{2,1,0:T(8,128)(2,1)} %param.6), kind=kOutput, calls=%fused_computation.2 | convolution fusion | flops 12884901888 | bytes 29360128 | tf_op jit(solution)/shard_map/dot_general | solution.py:28
  101.8 15.7 %all-gather.5.cloned.1.call-done = bf16[768,1024]{1,0:T(8,128)(2,1)} async-done(((bf16[192,1024]{1,0:T(8,128)(2,1)}), bf16[768,1024]{1,0:T(8,128)(2,1)}) %all-gather.5.cloned.1.call-update) | async-done | bytes 1572880 | tf_op jit(solution)/shard_map/all_gather | solution.py:26
  117.5 10.8 %multiply_convert_fusion = bf16[768,2048]{1,0:T(8,128)(2,1)} fusion(f32[768,2048]{1,0:T(8,128)} %fusion.2, bf16[768,1024]{1,0:T(8,128)(2,1)} %all-gather.5.cloned.1.call-done, bf16[1,2048,1024]{2,1,0:T(8,128)(2,1)} %param.7), kind=kOutput, calls=%fused_computation.4 | convolution fusion | flops 3235381248 | bytes 15204352 | tf_op jit(solution)/shard_map/dot_general | solution.py:34
  128.3 12.8 %fusion.4 = bf16[192,4096]{1,0:T(8,128)(2,1)} fusion(bf16[1,4096,2048]{2,1,0:T(8,128)(2,1)} %param.6, bf16[768,2048]{1,0:T(8,128)(2,1)} %multiply_convert_fusion, s32[]{:T(128)S(6)} %select_n.10), kind=kOutput, calls=%fused_computation.5 | convolution fusion | flops 3222011904 | bytes 19136516 | tf_op jit(solution)/shard_map/dot_general | solution.py:41
  141.1 0.0 reduce-scatter.2.cloned.1.call-update
  141.1 3.7 %fusion.20 = bf16[1,192,1024]{2,1,0:T(8,128)(2,1)S(1)} fusion(bf16[1,2048,1024]{2,1,0:T(8,128)(2,1)} %param.7, f32[768,2048]{1,0:T(8,128)} %fusion.2, s32[]{:T(128)S(6)} %select_n.10), kind=kOutput, calls=%fused_computation.21 | convolution fusion | flops 807469056 | bytes 6160388 | tf_op jit(solution)/shard_map/dot_general | solution.py:31
  144.8 0.6 copy.43
  145.4 0.5 broadcast.9
  145.9 2.9 %reduce = bf16[192,1024]{1,0:T(8,128)(2,1)S(1)} reduce(bf16[192,1,1024]{2,1,0:T(2,128)(2,1)S(1)} %bitcast.56, bf16[]{:T(256)} %broadcast.9), dimensions={1}, to_apply=%bitcast.55.reduce_sub_computation | reduce | bytes 786434
  148.9 1.2 reshape.24
  150.1 5.0 %all-to-all-start = ((bf16[8,2,12288]{2,1,0:T(2,128)(2,1)}), bf16[8,2,12288]{2,1,0:T(2,128)(2,1)S(1)}, u32[]{:S(2)}, u32[]{:S(2)}) async-start(bf16[8,2,12288]{2,1,0:T(2,128)(2,1)} %reshape.24), calls=%async_computation | async-start | bytes 786432 | tf_op jit(solution)/shard_map/all_to_all | solution.py:32
  155.1 0.0 copy-start.2
  155.1 8.0 %convert_bitcast_fusion = bf16[1,1024,2048]{2,1,0:T(8,128)(2,1)} fusion(bf16[768,2048]{1,0:T(8,128)(2,1)} %multiply_convert_fusion, bf16[768,4096]{1,0:T(8,128)(2,1)} %all-gather.3.cloned.1.call-done, s32[]{:T(128)S(6)} %select_n.11), kind=kOutput, calls=%fused_computation.10 | convolution fusion | flops 3223322624 | bytes 8912900 | tf_op jit(solution)/shard_map/dot_general | solution.py:59
  163.1 0.0 copy-done.2
  163.1 3.5 %fusion.14 = bf16[1,512,1024]{2,1,0:T(8,128)(2,1)} fusion(bf16[768,1024]{1,0:T(8,128)(2,1)S(1)} %copy-done.2, f32[768,2048]{1,0:T(8,128)} %fusion.2, s32[]{:T(128)S(6)} %select_n.12), kind=kOutput, calls=%fused_computation.15 | convolution fusion | flops 807796736 | bytes 4194308 | tf_op jit(solution)/shard_map/dot_general | solution.py:64
  166.5 0.0 all-to-all-done
  166.5 0.4 reshape.25
  166.9 0.1 copy.37
  167.1 0.4 fusion.23
  167.4 0.7 copy.35
  168.1 4.2 %all-to-all-start.3 = ((bf16[8,24,8]{1,2,0:T(8,128)(2,1)}), bf16[8,24,8]{1,2,0:T(8,128)(2,1)S(1)}, u32[]{:S(2)}, u32[]{:S(2)}) async-start(bf16[8,24,8]{1,2,0:T(8,128)(2,1)} %copy.35), calls=%async_computation.4 | async-start | bytes 32768 | tf_op jit(solution)/shard_map/all_to_all | solution.py:55
  172.3 1.1 fusion.18
  173.5 2.1 %all-to-all-done.3 = bf16[8,24,8]{1,2,0:T(8,128)(2,1)S(1)} async-done(((bf16[8,24,8]{1,2,0:T(8,128)(2,1)}), bf16[8,24,8]{1,2,0:T(8,128)(2,1)S(1)}, u32[]{:S(2)}, u32[]{:S(2)}) %all-to-all-start.3) | async-done | bytes 3104 | tf_op jit(solution)/shard_map/all_to_all | solution.py:55
  175.6 0.7 squeeze.19
  176.3 3.4 %reduce-scatter.2.cloned.1.call-done = bf16[24,4096]{1,0:T(8,128)(2,1)} async-done(((bf16[192,4096]{1,0:T(8,128)(2,1)}), bf16[24,4096]{1,0:T(8,128)(2,1)}) %reduce-scatter.2.cloned.1.call-update) | async-done | bytes 196624 | tf_op jit(solution)/shard_map/reduce_scatter | solution.py:40
  (1 shorter events, 0.0 us)
Async XLA Ops:
  7.2 9.7 %copy-start = (bf16[24,8,1024]{2,1,0:T(8,128)(2,1)S(1)}, bf16[24,8,1024]{2,1,0:T(8,128)(2,1)}, u32[]{:S(2)}) copy-start(bf16[24,8,1024]{2,1,0:T(8,128)(2,1)} %param.9) | copy-start | bytes 1179652
  7.2 74.4 %all-gather.3.cloned.1.call-start = ((), (), s32[]{:S(2)}) async-start(), calls=%async_computation.5 | async-start | bytes 6488064 | tf_op jit(solution)/shard_map/all_gather | solution.py:20
  18.1 11.9 %all-to-all-start.2 = ((bf16[8,24,1024]{2,1,0:T(8,128)(2,1)}), bf16[8,24,1024]{2,1,0:T(8,128)(2,1)S(1)}, u32[]{:S(2)}, u32[]{:S(2)}) async-start(bf16[8,24,1024]{2,1,0:T(8,128)(2,1)} %copy.33), calls=%async_computation.2 | async-start | bytes 786432 | tf_op jit(solution)/shard_map/all_to_all | solution.py:25
  23.2 94.3 %all-gather.5.cloned.1.call-start = ((), (), s32[]{:S(2)}) async-start(), calls=%async_computation.6 | async-start | bytes 1966080 | tf_op jit(solution)/shard_map/all_gather | solution.py:26
  30.0 0.7 copy-start.1
  30.7 148.9 %reduce-scatter.2.cloned.1.call-start = ((), (), s32[]{:S(2)}) async-start(), calls=%async_computation.7 | async-start | bytes 1769472 | tf_op jit(solution)/shard_map/reduce_scatter | solution.py:40
  150.1 16.5 %all-to-all-start = ((bf16[8,2,12288]{2,1,0:T(2,128)(2,1)}), bf16[8,2,12288]{2,1,0:T(2,128)(2,1)S(1)}, u32[]{:S(2)}, u32[]{:S(2)}) async-start(bf16[8,2,12288]{2,1,0:T(2,128)(2,1)} %reshape.24), calls=%async_computation | async-start | bytes 786432 | tf_op jit(solution)/shard_map/all_to_all | solution.py:32
  155.1 8.0 %copy-start.2 = (bf16[768,1024]{1,0:T(8,128)(2,1)S(1)}, bf16[768,1024]{1,0:T(8,128)(2,1)}, u32[]{:S(2)}) copy-start(bf16[768,1024]{1,0:T(8,128)(2,1)} %all-gather.5.cloned.1.call-done) | copy-start | bytes 4718596
  168.1 7.5 %all-to-all-start.3 = ((bf16[8,24,8]{1,2,0:T(8,128)(2,1)}), bf16[8,24,8]{1,2,0:T(8,128)(2,1)S(1)}, u32[]{:S(2)}, u32[]{:S(2)}) async-start(bf16[8,24,8]{1,2,0:T(8,128)(2,1)} %copy.35), calls=%async_computation.4 | async-start | bytes 32768 | tf_op jit(solution)/shard_map/all_to_all | solution.py:55
Sparse Core Ops, SparseCore 0:
  10.9 70.7 all-gather.2
  83.7 33.7 all-gather.4
  141.2 38.3 reduce-scatter.1

commit v2 on v1

v2 whole, which is shorter than its diff:
```python
import functools

import jax
import jax.numpy as jnp
from jax import lax
from jax.experimental import pallas as pl
from jax.experimental.pallas import tpu as pltpu
from jax.sharding import PartitionSpec as P

F32 = jnp.float32
BF16 = jnp.bfloat16


MESH = pl.DeviceIdType.MESH


def gather_kernel(n_e, n_d, trunk, gates, cot, first, second, rows, d_out, pre, gate_each,
                  outs, weights, later, hidden, made, m_send, m_recv, later_sem, piece, block, tall, w_sem, load_sem, store_sem,
                  g_send, g_recv, t_send, t_recv, o_send, o_recv, z_send, z_recv,
                  own_sem):
    e = lax.axis_index("expert")
    z = lax.axis_index("dp")
    partner = e + 1 - 2 * lax.rem(e, 2)
    pairs = n_e // 2

    def plane(s):
        return lax.rem(e + s, n_e)

    def along(i):
        return lax.rem(z + i, n_d)

    def remote(src, dst, send, recv, where):
        return pltpu.make_async_remote_copy(
            src_ref=src, dst_ref=dst, send_sem=send, recv_sem=recv,
            device_id=where, device_id_type=MESH)

    load_weights = pltpu.make_async_copy(first, weights, w_sem)
    load_weights.start()
    load_later = pltpu.make_async_copy(second, later, later_sem)
    load_later.start()

    barrier = pltpu.get_barrier_semaphore()
    for s in range(1, n_e):
        pl.semaphore_signal(barrier, inc=1, device_id={"expert": plane(s)}, device_id_type=MESH)
    for i in range(1, n_d):
        pl.semaphore_signal(barrier, inc=1, device_id={"dp": along(i)}, device_id_type=MESH)
    pl.semaphore_wait(barrier, n_e - 1 + n_d - 1)

    sent = []

    def go(copy):
        copy.start()
        sent.append(copy)

    for s in range(1, n_e):
        j = plane(s)
        go(remote(gates.at[j], gate_each.at[e], g_send.at[s], g_recv.at[e], {"expert": j}))
    own_gate = pltpu.make_async_copy(gates.at[e], gate_each.at[e], own_sem.at[0])
    own_gate.start()
    own_rows = pltpu.make_async_copy(trunk, rows.at[z, e], own_sem.at[1])
    own_rows.start()

    def spread(i):
        zi = along(i)
        src = trunk if i == 0 else rows.at[zi, e]
        for s in range(1, pairs):
            go(remote(src, rows.at[zi, e], t_send.at[i, s], t_recv.at[zi, e],
                      {"expert": plane(2 * s)}))
        go(remote(src, rows.at[zi, e], t_send.at[i, 0], t_recv.at[zi, e], {"expert": partner}))

    def arrived(zi, j):
        remote(trunk, rows.at[zi, j], t_send.at[0, 0], t_recv.at[zi, j],
               {"expert": partner}).wait_recv()

    for i in range(1, n_d):
        go(remote(trunk, rows.at[z, e], t_send.at[i, n_e - 1], t_recv.at[z, e], {"dp": along(i)}))
    spread(0)

    for s in range(1, n_e):
        j = plane(s)
        remote(gates.at[j], gate_each.at[j], g_send.at[0], g_recv.at[j], {"expert": j}).wait_recv()
    own_gate.wait()
    tasks = cot.shape[0]

    @pl.loop(0, n_e)
    def _(j):
        weight = gate_each[j]
        total = weight[:, 0:1] * cot[0].astype(F32)
        for t in range(1, tasks):
            total = total + weight[:, t:t + 1] * cot[t].astype(F32)
        piece[j] = total.astype(BF16)

    own_piece = pltpu.make_async_copy(piece.at[e], d_out.at[z, e], own_sem.at[2])
    own_piece.start()
    for s in range(1, n_e):
        j = plane(s)
        go(remote(piece.at[j], d_out.at[z, e], o_send.at[s], o_recv.at[e], {"expert": j}))

    def send_outputs():
        own_made.start()
        for s in range(1, n_e):
            j = plane(s)
            go(remote(made.at[j], outs.at[e], m_send.at[s], m_recv.at[e], {"expert": j}))

    own_made = pltpu.make_async_copy(made.at[e], outs.at[e], own_sem.at[3])
    stores = []
    for i in range(n_d):
        zi = along(i)
        if i + 1 < n_d:
            arrived(along(i + 1), e)
            spread(i + 1)
        if i == 1:
            send_outputs()
        if i == 0:
            for s in range(1, n_e):
                j = plane(s)
                remote(piece.at[j], d_out.at[z, j], o_send.at[0], o_recv.at[j],
                       {"expert": j}).wait_recv()
            own_piece.wait()
            for k in range(1, n_d):
                go(remote(d_out.at[z], d_out.at[z], z_send.at[k], z_recv.at[z], {"dp": along(k)}))
            own_rows.wait()
        for s in range(1, pairs):
            j = plane(2 * s)
            arrived(zi, j)
            go(remote(rows.at[zi, j], rows.at[zi, j], t_send.at[i, pairs - 1 + s],
                      t_recv.at[zi, j], {"expert": partner}))
        for s in range(pairs):
            arrived(zi, lax.rem(partner + 2 * s, n_e))
        load = pltpu.make_async_copy(rows.at[zi], block, load_sem)
        load.start()
        if i == 0:
            load_weights.wait()
        else:
            stores[-1].wait()
        load.wait()
        height = block.shape[0] * block.shape[1]
        tile = 256
        left = block[...].reshape(height, block.shape[2])

        @pl.loop(0, tall.shape[1] // tile)
        def _(c):
            here = pl.ds(pl.multiple_of(c * tile, tile), tile)
            value = jnp.dot(left, weights[:, here], preferred_element_type=F32)
            tall[:, here] = value
            if i == 0:
                hidden[:, here] = (value * jax.nn.sigmoid(value)).astype(BF16)

        store = pltpu.make_async_copy(tall, pre.at[zi], store_sem)
        store.start()
        stores.append(store)
        if i == 0:
            load_later.wait()

            @pl.loop(0, made.shape[2] // tile)
            def _(c):
                here = pl.ds(pl.multiple_of(c * tile, tile), tile)
                value = jnp.dot(hidden[...], later[:, here], preferred_element_type=F32)
                made[:, :, here] = value.astype(BF16).reshape(n_e, -1, tile)

    stores[-1].wait()
    if n_d == 1:
        send_outputs()
    own_made.wait()
    for s in range(1, n_e):
        j = plane(s)
        remote(made.at[j], outs.at[j], m_send.at[0], m_recv.at[j], {"expert": j}).wait_recv()
    for i in range(1, n_d):
        zi = along(i)
        remote(d_out.at[zi], d_out.at[zi], z_send.at[0], z_recv.at[zi], {"dp": zi}).wait_recv()
    for copy in sent:
        copy.wait_send()


def gather_all(trunk, gates, cot, first, second):
    n_e, n_d = lax.axis_size("expert"), lax.axis_size("dp")
    share, depth = trunk.shape
    width = first.shape[1]
    out = cot.shape[2]
    anywhere = pl.BlockSpec(memory_space=pl.ANY)
    hbm = pl.BlockSpec(memory_space=pltpu.HBM)
    vmem = pl.BlockSpec(memory_space=pltpu.VMEM)
    dma = pltpu.SemaphoreType.DMA
    return pl.pallas_call(
        functools.partial(gather_kernel, n_e, n_d),
        out_shape=(
            jax.ShapeDtypeStruct((n_d, n_e, share, depth), BF16),
            jax.ShapeDtypeStruct((n_d, n_e, share, out), BF16),
            jax.ShapeDtypeStruct((n_d, n_e * share, width), F32),
            jax.ShapeDtypeStruct(gates.shape, F32),
            jax.ShapeDtypeStruct((n_e, share, out), BF16),
        ),
        in_specs=[vmem, vmem, vmem, hbm, hbm],
        out_specs=(hbm, hbm, hbm, vmem, hbm),
        scratch_shapes=[
            pltpu.VMEM(first.shape, BF16),
            pltpu.VMEM(second.shape, BF16),
            pltpu.VMEM((n_e * share, width), BF16),
            pltpu.VMEM((n_e, share, out), BF16),
            dma((n_e,)), dma((n_e,)), dma,
            pltpu.VMEM((n_e, share, out), BF16),
            pltpu.VMEM((n_e, share, depth), BF16),
            pltpu.VMEM((n_e * share, width), F32),
            dma, dma, dma,
            dma((n_e,)), dma((n_e,)),
            dma((n_d, n_e)), dma((n_d, n_e)),
            dma((n_e,)), dma((n_e,)),
            dma((n_d,)), dma((n_d,)),
            dma((4,)),
        ],
        compiler_params=pltpu.CompilerParams(
            collective_id=0, has_side_effects=True, vmem_limit_bytes=48 * 1024 * 1024),
    )(trunk, gates, cot, first, second)


def return_kernel(n_e, d_pre, first, d_gate, d_trunk, gate_back, weights, part, got,
                  w_sem, p_send, p_recv, g_send, g_recv, own_sem):
    e = lax.axis_index("expert")
    tiles, tile, _ = weights.shape

    def plane(s):
        return lax.rem(e + s, n_e)

    def remote(src, dst, send, recv, j):
        return pltpu.make_async_remote_copy(
            src_ref=src, dst_ref=dst, send_sem=send, recv_sem=recv,
            device_id={"expert": j}, device_id_type=MESH)

    def load(c):
        return pltpu.make_async_copy(first.at[c], weights.at[c], w_sem.at[c])

    for c in range(tiles):
        load(c).start()
    barrier = pltpu.get_barrier_semaphore()
    for s in range(1, n_e):
        pl.semaphore_signal(barrier, inc=1, device_id={"expert": plane(s)}, device_id_type=MESH)
    pl.semaphore_wait(barrier, n_e - 1)

    own = pltpu.make_async_copy(d_gate.at[e], gate_back.at[e], own_sem)
    own.start()

    def gate_out(s):
        j = plane(s)
        return remote(d_gate.at[j], gate_back.at[e], g_send.at[s], g_recv.at[e], j)

    def part_out(c, s):
        j = plane(s)
        return remote(part.at[c, j], got.at[c, e], p_send.at[c, s], p_recv.at[c, e], j)

    for s in range(1, n_e):
        gate_out(s).start()

    def compute(c):
        load(c).wait()
        value = lax.dot_general(
            d_pre[...], weights[c], (((1,), (1,)), ((), ())), preferred_element_type=F32)
        part[c] = value.astype(BF16).reshape(n_e, -1, tile)

    def send(c):
        for s in range(1, n_e):
            part_out(c, s).start()

    compute(0)

    @pl.loop(1, tiles)
    def _(c):
        send(c - 1)
        compute(c)

    send(tiles - 1)

    @pl.loop(0, tiles)
    def _(c):
        total = part[c, e].astype(F32)
        for s in range(1, n_e):
            j = plane(s)
            remote(part.at[c, j], got.at[c, j], p_send.at[c, 0], p_recv.at[c, j], j).wait_recv()
            total = total + got[c, j].astype(F32)
        d_trunk[:, pl.ds(pl.multiple_of(c * tile, tile), tile)] = total.astype(BF16)

    own.wait()
    for s in range(1, n_e):
        j = plane(s)
        remote(d_gate.at[j], gate_back.at[j], g_send.at[0], g_recv.at[j], j).wait_recv()
    for s in range(1, n_e):
        gate_out(s).wait_send()

    @pl.loop(0, tiles)
    def _(c):
        for s in range(1, n_e):
            part_out(c, s).wait_send()


def return_all(d_pre, first, d_gate):
    n_e = lax.axis_size("expert")
    tile = 512
    depth, width = first.shape
    tiles = depth // tile
    share = d_pre.shape[0] // n_e
    hbm = pl.BlockSpec(memory_space=pltpu.HBM)
    vmem = pl.BlockSpec(memory_space=pltpu.VMEM)
    dma = pltpu.SemaphoreType.DMA
    return pl.pallas_call(
        functools.partial(return_kernel, n_e),
        out_shape=(
            jax.ShapeDtypeStruct((share, depth), BF16),
            jax.ShapeDtypeStruct(d_gate.shape, F32),
        ),
        in_specs=[vmem, hbm, vmem],
        out_specs=(vmem, vmem),
        scratch_shapes=[
            pltpu.VMEM((tiles, tile, width), BF16),
            pltpu.VMEM((tiles, n_e, share, tile), BF16),
            pltpu.VMEM((tiles, n_e, share, tile), BF16),
            dma((tiles,)),
            dma((tiles, n_e)), dma((tiles, n_e)),
            dma((n_e,)), dma((n_e,)), dma,
        ],
        compiler_params=pltpu.CompilerParams(
            collective_id=1, has_side_effects=True, vmem_limit_bytes=48 * 1024 * 1024),
    )(d_pre, first.reshape(tiles, tile, width), d_gate)


def on_device(trunk, w_first, w_second, gates, d_mixed):
    rank = lax.axis_index("dp")
    first = w_first[0]
    second = w_second[0]
    gate_here = gates[0]
    n_dp = lax.axis_size("dp")
    depth = first.shape[0] // n_dp
    units = second.shape[0] // n_dp
    group = gate_here.shape[1]

    n_e = lax.axis_size("expert")
    gate_parts = gate_here.T.astype(F32).reshape(n_e, -1, gate_here.shape[0])
    rows_all, d_output_all, pre, gates_each, outs_each = gather_all(
        trunk, gate_parts, jnp.transpose(d_mixed, (1, 0, 2)), first, second)
    rows_all = rows_all.reshape(-1, trunk.shape[1])
    d_output_all = d_output_all.reshape(-1, second.shape[1])
    pre = pre.reshape(-1, first.shape[1])
    gates_each = gates_each.astype(BF16)
    d_hidden = lax.dot_general(
        d_output_all, second, (((1,), (1,)), ((), ())), preferred_element_type=F32
    )
    sig = jax.nn.sigmoid(pre)
    d_pre = (d_hidden * sig * (1.0 + pre * (1.0 - sig))).astype(BF16)
    d_pre_here = lax.dynamic_slice_in_dim(d_pre, rank * group, group, 0)
    mixed = jnp.einsum(
        "ert,ero->rto", gates_each, outs_each, preferred_element_type=F32
    ).astype(BF16)
    d_gate_each = jnp.einsum(
        "rto,ero->ert", d_mixed, outs_each, preferred_element_type=F32
    ).astype(BF16)
    d_trunk, back_gate = return_all(d_pre_here, first, d_gate_each.astype(F32))
    d_gate = back_gate.reshape(group, -1).T.astype(BF16)[None]

    columns = lax.dynamic_slice_in_dim(rows_all, rank * depth, depth, 1)
    d_first = lax.dot_general(
        columns, d_pre, (((0,), (0,)), ((), ())), preferred_element_type=F32
    ).astype(BF16)
    some_pre = lax.dynamic_slice_in_dim(pre, rank * units, units, 1)
    some_hidden = jax.nn.silu(some_pre).astype(BF16)
    d_second = lax.dot_general(
        some_hidden, d_output_all, (((0,), (0,)), ((), ())), preferred_element_type=F32
    ).astype(BF16)
    return (mixed, d_trunk, d_gate, d_first[None], d_second[None])


def solution(mesh):
    in_specs = (
        P(("dp", "expert"), None),
        P("expert", None, None),
        P("expert", None, None),
        P("expert", None, "dp"),
        P(("dp", "expert"), None, None),
    )
    out_specs = (
        P(("dp", "expert"), None, None),
        P(("dp", "expert"), None),
        P("expert", None, "dp"),
        P("expert", "dp", None),
        P("expert", "dp", None),
    )
    return jax.shard_map(
        on_device, mesh=mesh, in_specs=in_specs, out_specs=out_specs, check_vma=False
    )
```

time: 189 us -> 129 us (0.68); the launches traced: 186 us -> 129 us
  Pallas kernels: 0 us -> 105 us
  waiting for transfers between devices: 79.6 us -> 0 us
  matrix products: 60.7 us -> 18.3 us
  starting transfers between devices: 14.4 us -> 0 us
  between operations: 13.8 us -> 0.73 us
  blocking collectives: 7.8 us -> 0 us
  local copies, waits for them, and re-layouts: 7.06 us -> 3.86 us
  other arithmetic: 2.92 us -> 0.72 us
    pallas_call x0 -> x2, Pallas kernels: none -> 105 us  [the longest x1 80.8 us: gather_all(): pl.pallas_call(functools.partial(gather_kernel, n_e, n_d), out_shape=(jax...]
    all_gather x2 -> x0, waiting for transfers between devices: 66.5 us -> none  [the longest x1 50.8 us: on_device(): rows_all = lax.all_gather(trunk, ('dp', 'expert'), axis=0, tiled=True)]
    dot_general x4 -> x0, matrix products: 37 us -> none  [the longest x1 20.2 us: on_device(): pre = jnp.dot(rows_all, first, preferred_element_type=F32)]
    all_to_all x3 -> x0, starting transfers between devices: 14.3 us -> none  [the longest x1 5.1 us: on_device(): lax.all_to_all(d_out_each, 'expert', split_axis=0, concat_axis=1, tiled=T...]
    all_to_all x3 -> x0, waiting for transfers between devices: 8.95 us -> none  [the longest x1 6.8 us: on_device(): lax.all_to_all(d_out_each, 'expert', split_axis=0, concat_axis=1, tiled=T...]
    all_to_all x1 -> x0, blocking collectives: 7.8 us -> none  [on_device(): lax.all_to_all(gate_here.T[None], 'expert', split_axis=1, concat_axis=0,...]
    dot_general x1, matrix products: 10.8 us -> 6.74 us  [on_device(): lax.dot_general(d_output_all, second, (((1,), (1,)), ((), ())), preferred...]
    reduce_scatter x1 -> x0, waiting for transfers between devices: 3.39 us -> none  [on_device(): lax.psum_scatter(lax.dot_general(d_pre_here, first, (((1,), (1,)), ((), (...]
  transfers between devices with their start and end apart: 6 -> 0, of which waited for: 5 -> 0; matrix products, arithmetic and copies ran while one was open for 25% -> 0% of each run, Pallas kernels for 0% -> 0%
where the time goes in v2:
time: 129 us
  Pallas kernels  105 us (81%)
  matrix products  18.3 us (14%)
  local copies, waits for them, and re-layouts  3.86 us (3%)
    pallas_call x1, Pallas kernels, gather_all(): pl.pallas_call(functools.partial(gather_kernel, n_e, n_d), out_shape=(jax...  80.8 us
    pallas_call x1, Pallas kernels, return_all(): pl.pallas_call(functools.partial(return_kernel, n_e), out_shape=(jax.Shap...  24.2 us
    dot_general x1, matrix products, on_device(): lax.dot_general(d_output_all, second, (((1,), (1,)), ((), ())), preferred...  6.74 us
    dot_general x1, matrix products, on_device(): lax.dot_general(columns, d_pre, (((0,), (0,)), ((), ())), preferred_eleme...  6.44 us
    dot_general x1, matrix products, on_device(): lax.dot_general(some_hidden, d_output_all, (((0,), (0,)), ((), ())), pref...  3.58 us
    unnamed x8, local copies, waits for them, and re-layouts  2.83 us

profile of v2, /device:TPU:11, one launch (start us, length us, event | category | flops | bytes accessed | tf_op | source)
XLA Modules:
  0.0 128.6 jit_solution(11128073598478933251)
XLA Ops:
  0.6 0.7 convert_bitcast_fusion.2
  1.3 0.1 copy.17
  1.4 1.2 copy.32
  2.7 0.0 copy-start
  2.7 0.9 copy-done
  3.6 0.0 copy-start.2
  3.6 80.8 %shard_map.92 = (bf16[4,8,24,4096]{3,2,1,0:T(8,128)(2,1)}, bf16[4,8,24,1024]{3,2,1,0:T(8,128)(2,1)S(1)}, f32[4,192,2048]{2,1,0:T(8,128)}, f32[8,24,8]{2,1,0:T(8,128)S(1)}, bf16[8,24,1024]{2,1,0:T(8,128)(2,1)S(1)}) custom-call(bf16[24,4096]{1,0:T(8,128)(2,1)S(1)} %copy-done, f32[8,24,8]{2,1,0:T(8,128)S(1)} %bitcast.32, bf16[8,24,1024]{2,1,0:T(8,128)(2,1)S(1)} %bitcast.31, ...), custom_call_target="tpu_custom_call" | custom-call | tf_op jit(solution)/shard_map/pallas_call | solution.py:184
  84.4 0.0 copy-done.2
  84.4 0.4 fusion.3
  84.8 1.1 convolution_convert_fusion.1
  85.9 0.1 copy.22
  86.0 0.1 copy.23
  86.1 0.0 copy-start.1
  86.1 3.6 %fusion.1 = bf16[1,512,1024]{2,1,0:T(8,128)(2,1)} fusion(bf16[768,1024]{1,0:T(8,128)(2,1)S(1)} %bitcast.33, f32[768,2048]{1,0:T(8,128)} %bitcast.41, s32[]{:T(128)S(6)} %select_n.11), kind=kOutput, calls=%fused_computation.5 | convolution fusion | flops 807796736 | bytes 4194308 | tf_op jit(solution)/shard_map/dot_general | solution.py:363
  89.7 0.0 copy-done.1
  89.7 6.7 %multiply_convert_fusion = bf16[768,2048]{1,0:T(8,128)(2,1)S(1)} fusion(f32[768,2048]{1,0:T(8,128)} %bitcast.42, bf16[768,1024]{1,0:T(8,128)(2,1)S(1)} %bitcast.34, bf16[1,2048,1024]{2,1,0:T(8,128)(2,1)S(1)} %copy-done.1), kind=kOutput, calls=%fused_computation | convolution fusion | flops 3235381248 | bytes 15204352 | tf_op jit(solution)/shard_map/dot_general | solution.py:342
  96.5 6.4 %convert_bitcast_fusion = bf16[1,1024,2048]{2,1,0:T(8,128)(2,1)} fusion(bf16[768,2048]{1,0:T(8,128)(2,1)S(1)} %multiply_convert_fusion, bf16[768,4096]{1,0:T(8,128)(2,1)} %bitcast.40, s32[]{:T(128)S(6)} %select_n.10), kind=kOutput, calls=%fused_computation.1 | convolution fusion | flops 3223322624 | bytes 8912900 | tf_op jit(solution)/shard_map/dot_general | solution.py:358
  102.9 0.1 constant_dynamic-slice_fusion.d_pre
  103.0 24.2 %shard_map.93 = (bf16[24,4096]{1,0:T(8,128)(2,1)S(1)}, f32[8,24,8]{2,1,0:T(8,128)S(1)}) custom-call(bf16[192,2048]{1,0:T(8,128)(2,1)S(1)} %constant_dynamic-slice_fusion.d_pre, bf16[8,512,2048]{2,1,0:T(8,128)(2,1)} %bitcast.36, f32[8,24,8]{2,1,0:T(8,128)S(1)} %convert_bitcast_fusion.1.d_gate), custom_call_target="tpu_custom_call" | custom-call | tf_op jit(solution)/shard_map/pallas_call | solution.py:303
  127.2 0.7 copy.24
  127.9 0.7 copy.34
  (3 shorter events, 0.0 us)
Async XLA Ops:
  2.7 0.9 copy-start
  3.6 80.8 %copy-start.2 = (bf16[24,8,1024]{2,1,0:T(8,128)(2,1)S(1)}, bf16[24,8,1024]{2,1,0:T(8,128)(2,1)}, u32[]{:S(2)}) copy-start(bf16[24,8,1024]{2,1,0:T(8,128)(2,1)} %param.9) | copy-start | bytes 1179652
  86.1 3.6 %copy-start.1 = (bf16[1,2048,1024]{2,1,0:T(8,128)(2,1)S(1)}, bf16[1,2048,1024]{2,1,0:T(8,128)(2,1)}, u32[]{:S(2)}) copy-start(bf16[1,2048,1024]{2,1,0:T(8,128)(2,1)} %param.7) | copy-start | bytes 12582916

commit v3 on v2

--- a/solution.py
+++ b/solution.py
@@ -213,9 +213,11 @@
     )(trunk, gates, cot, first, second)
 
 
-def return_kernel(n_e, d_pre, first, d_gate, d_trunk, gate_back, weights, part, got,
-                  w_sem, p_send, p_recv, g_send, g_recv, own_sem):
+def return_kernel(n_e, d_pre, first, d_gate, d_trunk, gate_back, weights, part, near, pair, got,
+                  w_sem, n_send, n_recv, p_send, p_recv, g_send, g_recv, own_sem):
     e = lax.axis_index("expert")
+    core, seat, pairs = lax.rem(e, 2), e // 2, n_e // 2
+    partner = e + 1 - 2 * core
     tiles, tile, _ = weights.shape
 
     def plane(s):
@@ -243,9 +245,13 @@
         j = plane(s)
         return remote(d_gate.at[j], gate_back.at[e], g_send.at[s], g_recv.at[e], j)
 
+    def near_out(c):
+        return remote(part.at[c, :, 1 - core], near.at[c], n_send.at[c], n_recv.at[c], partner)
+
     def part_out(c, s):
-        j = plane(s)
-        return remote(part.at[c, j], got.at[c, e], p_send.at[c, s], p_recv.at[c, e], j)
+        k = lax.rem(seat + s, pairs)
+        return remote(pair.at[c, k], got.at[c, seat], p_send.at[c, s], p_recv.at[c, seat],
+                      2 * k + core)
 
     for s in range(1, n_e):
         gate_out(s).start()
@@ -254,28 +260,41 @@
         load(c).wait()
         value = lax.dot_general(
             d_pre[...], weights[c], (((1,), (1,)), ((), ())), preferred_element_type=F32)
-        part[c] = value.astype(BF16).reshape(n_e, -1, tile)
+        part[c] = value.astype(BF16).reshape(pairs, 2, -1, tile)
+
+    def combine(c):
+        near_out(c).wait_recv()
+        pair[c] = (part[c, :, core].astype(F32) + near[c].astype(F32)).astype(BF16)
 
     def send(c):
-        for s in range(1, n_e):
+        for s in range(1, pairs):
             part_out(c, s).start()
 
     compute(0)
-
-    @pl.loop(1, tiles)
+    near_out(0).start()
+    compute(1)
+    combine(0)
+
+    @pl.loop(2, tiles)
     def _(c):
-        send(c - 1)
+        near_out(c - 1).start()
+        send(c - 2)
         compute(c)
-
+        combine(c - 1)
+
+    near_out(tiles - 1).start()
+    send(tiles - 2)
+    combine(tiles - 1)
     send(tiles - 1)
 
     @pl.loop(0, tiles)
     def _(c):
-        total = part[c, e].astype(F32)
-        for s in range(1, n_e):
-            j = plane(s)
-            remote(part.at[c, j], got.at[c, j], p_send.at[c, 0], p_recv.at[c, j], j).wait_recv()
-            total = total + got[c, j].astype(F32)
+        total = pair[c, seat].astype(F32)
+        for s in range(1, pairs):
+            k = lax.rem(seat + s, pairs)
+            remote(pair.at[c, k], got.at[c, k], p_send.at[c, 0], p_recv.at[c, k],
+                   2 * k + core).wait_recv()
+            total = total + got[c, k].astype(F32)
         d_trunk[:, pl.ds(pl.multiple_of(c * tile, tile), tile)] = total.astype(BF16)
 
     own.wait()
@@ -287,7 +306,8 @@
 
     @pl.loop(0, tiles)
     def _(c):
-        for s in range(1, n_e):
+        near_out(c).wait_send()
+        for s in range(1, pairs):
             part_out(c, s).wait_send()
 
 
@@ -310,10 +330,12 @@
         out_specs=(vmem, vmem),
         scratch_shapes=[
             pltpu.VMEM((tiles, tile, width), BF16),
-            pltpu.VMEM((tiles, n_e, share, tile), BF16),
-            pltpu.VMEM((tiles, n_e, share, tile), BF16),
-            dma((tiles,)),
-            dma((tiles, n_e)), dma((tiles, n_e)),
+            pltpu.VMEM((tiles, n_e // 2, 2, share, tile), BF16),
+            pltpu.VMEM((tiles, n_e // 2, share, tile), BF16),
+            pltpu.VMEM((tiles, n_e // 2, share, tile), BF16),
+            pltpu.VMEM((tiles, n_e // 2, share, tile), BF16),
+            dma((tiles,)), dma((tiles,)), dma((tiles,)),
+            dma((tiles, n_e // 2)), dma((tiles, n_e // 2)),
             dma((n_e,)), dma((n_e,)), dma,
         ],
         compiler_params=pltpu.CompilerParams(

time: 129 us -> 122 us (0.946)
  Pallas kernels: 105 us -> 96.8 us
    pallas_call x1, Pallas kernels: 24.2 us -> 16 us  [return_all(): pl.pallas_call(functools.partial(return_kernel, n_e), out_shape=(jax.Shap...]
where the time goes in v3:
time: 122 us; the launch traced here: 120 us
  Pallas kernels  96.8 us (79%)
  matrix products  18.3 us (15%)
  local copies, waits for them, and re-layouts  3.86 us (3%)
    pallas_call x1, Pallas kernels, gather_all(): pl.pallas_call(functools.partial(gather_kernel, n_e, n_d), out_shape=(jax...  80.8 us
    pallas_call x1, Pallas kernels, return_all(): pl.pallas_call(functools.partial(return_kernel, n_e), out_shape=(jax.Shap...  16 us
    dot_general x1, matrix products, on_device(): lax.dot_general(d_output_all, second, (((1,), (1,)), ((), ())), preferred...  6.74 us
    dot_general x1, matrix products, on_device(): lax.dot_general(columns, d_pre, (((0,), (0,)), ((), ())), preferred_eleme...  6.44 us
    dot_general x1, matrix products, on_device(): lax.dot_general(some_hidden, d_output_all, (((0,), (0,)), ((), ())), pref...  3.58 us
    unnamed x8, local copies, waits for them, and re-layouts  2.83 us

profile of v3, /device:TPU:11, one launch (start us, length us, event | category | flops | bytes accessed | tf_op | source)
XLA Modules:
  0.0 120.4 jit_solution(3503409141554923387)
XLA Ops:
  0.6 0.7 convert_bitcast_fusion.2
  1.3 0.1 copy.17
  1.4 1.2 %copy.32 = bf16[24,8,1024]{2,0,1:T(8,128)(2,1)S(1)} copy(bf16[24,8,1024]{2,1,0:T(8,128)(2,1)} %param.9) | data formatting | bytes 786432 | tf_op args[4]
  2.7 0.0 copy-start
  2.7 0.9 copy-done
  3.6 0.0 copy-start.2
  3.6 80.8 %shard_map.92 = (bf16[4,8,24,4096]{3,2,1,0:T(8,128)(2,1)}, bf16[4,8,24,1024]{3,2,1,0:T(8,128)(2,1)S(1)}, f32[4,192,2048]{2,1,0:T(8,128)}, f32[8,24,8]{2,1,0:T(8,128)S(1)}, bf16[8,24,1024]{2,1,0:T(8,128)(2,1)S(1)}) custom-call(bf16[24,4096]{1,0:T(8,128)(2,1)S(1)} %copy-done, f32[8,24,8]{2,1,0:T(8,128)S(1)} %bitcast.32, bf16[8,24,1024]{2,1,0:T(8,128)(2,1)S(1)} %bitcast.31, ...), custom_call_target="tpu_custom_call" | custom-call | tf_op jit(solution)/shard_map/pallas_call | solution.py:184
  84.4 0.0 copy-done.2
  84.4 0.4 fusion.3
  84.8 1.1 convolution_convert_fusion.1
  85.9 0.1 copy.22
  86.0 0.1 copy.23
  86.1 0.0 copy-start.1
  86.1 3.6 %fusion.1 = bf16[1,512,1024]{2,1,0:T(8,128)(2,1)} fusion(bf16[768,1024]{1,0:T(8,128)(2,1)S(1)} %bitcast.33, f32[768,2048]{1,0:T(8,128)} %bitcast.41, s32[]{:T(128)S(6)} %select_n.11), kind=kOutput, calls=%fused_computation.5 | convolution fusion | flops 807796736 | bytes 4194308 | tf_op jit(solution)/shard_map/dot_general | solution.py:385
  89.7 0.0 copy-done.1
  89.7 6.7 %multiply_convert_fusion = bf16[768,2048]{1,0:T(8,128)(2,1)S(1)} fusion(f32[768,2048]{1,0:T(8,128)} %bitcast.42, bf16[768,1024]{1,0:T(8,128)(2,1)S(1)} %bitcast.34, bf16[1,2048,1024]{2,1,0:T(8,128)(2,1)S(1)} %copy-done.1), kind=kOutput, calls=%fused_computation | convolution fusion | flops 3235381248 | bytes 15204352 | tf_op jit(solution)/shard_map/dot_general | solution.py:364
  96.5 6.4 %convert_bitcast_fusion = bf16[1,1024,2048]{2,1,0:T(8,128)(2,1)} fusion(bf16[768,2048]{1,0:T(8,128)(2,1)S(1)} %multiply_convert_fusion, bf16[768,4096]{1,0:T(8,128)(2,1)} %bitcast.40, s32[]{:T(128)S(6)} %select_n.10), kind=kOutput, calls=%fused_computation.1 | convolution fusion | flops 3223322624 | bytes 8912900 | tf_op jit(solution)/shard_map/dot_general | solution.py:380
  102.9 0.1 constant_dynamic-slice_fusion.d_pre
  103.0 16.0 %shard_map.93 = (bf16[24,4096]{1,0:T(8,128)(2,1)S(1)}, f32[8,24,8]{2,1,0:T(8,128)S(1)}) custom-call(bf16[192,2048]{1,0:T(8,128)(2,1)S(1)} %constant_dynamic-slice_fusion.d_pre, bf16[8,512,2048]{2,1,0:T(8,128)(2,1)} %bitcast.36, f32[8,24,8]{2,1,0:T(8,128)S(1)} %convert_bitcast_fusion.1.d_gate), custom_call_target="tpu_custom_call" | custom-call | tf_op jit(solution)/shard_map/pallas_call | solution.py:323
  119.0 0.7 copy.24
  119.7 0.7 copy.34
  (3 shorter events, 0.0 us)
Async XLA Ops:
  2.7 0.9 copy-start
  3.6 80.8 %copy-start.2 = (bf16[24,8,1024]{2,1,0:T(8,128)(2,1)S(1)}, bf16[24,8,1024]{2,1,0:T(8,128)(2,1)}, u32[]{:S(2)}) copy-start(bf16[24,8,1024]{2,1,0:T(8,128)(2,1)} %param.9) | copy-start | bytes 1179652
  86.1 3.6 %copy-start.1 = (bf16[1,2048,1024]{2,1,0:T(8,128)(2,1)S(1)}, bf16[1,2048,1024]{2,1,0:T(8,128)(2,1)}, u32[]{:S(2)}) copy-start(bf16[1,2048,1024]{2,1,0:T(8,128)(2,1)} %param.7) | copy-start | bytes 12582916
